TPU v7x, 256 devices: a whole 4x4x8 slice. The times are simulated.
256 devices in a mesh: layer: 4 (over x), row: 8 (over y, core), col: 8 (over z).
Axes of the slice: x: 4, y: 4, z: 8, core: 2. Of those that a mesh axis runs over, the one named last changes fastest.
Arguments:
- left_values: bfloat16 [8192, 4, 2048], P('row', 'layer', 'col'), may hold values from -22 to 22
- left_pattern: int32 [32, 4, 8], P('row', 'layer', 'col'), may hold values from 0 to 1, as said below
- right_values: bfloat16 [8192, 4, 2048], P(('layer', 'row'), None, 'col'), may hold values from -6 to 6
- right_pattern: int32 [32, 4, 8], P(('layer', 'row'), None, 'col'), may hold values from 0 to 1, as said below
Outputs:
- expanded: bfloat16 [8192, 4, 2048], P('row', 'layer', 'col')
Inputs may be any that keep to these rules, and one draw needn't show every extreme that they name: `left_pattern`: 1 marks a stored tile, 0 an absent one. `right_pattern`: 1 marks a stored tile, 0 an absent one.
All inputs are finite; a program needn't handle non-finite values.
Results may differ from a plain program's by a relative error of at most 0.001.
Values may be sent and summed in bfloat16 or wider, within the bound.
A program may use at most 64 MiB of HBM per device.

v0:
```python
import jax
import jax.numpy as jnp
from jax import lax
from jax.sharding import PartitionSpec as P


def expand_tiles(values, pattern):
    tile_rows, layers, tile_cols = pattern.shape
    tile_size = values.shape[0] // tile_rows
    blocks = values.reshape(tile_rows, tile_size, layers, tile_cols, tile_size)
    blocks = blocks * pattern[:, None, :, :, None].astype(values.dtype)
    return blocks.reshape(values.shape)


def per_device(left_values, left_pattern, right_values, right_pattern):
    left_block = expand_tiles(left_values, left_pattern)
    right_block = expand_tiles(right_values, right_pattern)
    rows_local = left_block.shape[0]
    columns_local = left_block.shape[2]
    left_flat = left_block.reshape(rows_local, columns_local)
    right_flat = right_block.reshape(right_block.shape[0], -1)
    right_all = lax.all_gather(right_flat, "row", axis=0, tiled=True)
    left_all = lax.all_gather(left_flat, "col", axis=1, tiled=True)
    partial = jnp.dot(left_all, right_all, preferred_element_type=jnp.float32)
    layers = lax.axis_size("layer")
    partial = jnp.stack(
        [partial[:, columns_local * l : columns_local * (l + 1)] for l in range(layers)], axis=0
    )
    product = lax.psum_scatter(partial, "layer", scatter_dimension=0, tiled=True)
    product = product.reshape(rows_local, 1, columns_local)
    squared = product * product
    column = lax.psum(jnp.sum(squared, axis=0, keepdims=True), "row")
    rows_total = rows_local * lax.axis_size("row")
    colmean = column / rows_total
    return (squared / (colmean + 1e-06)).astype(jnp.bfloat16)


def solution(mesh):
    return jax.shard_map(
        per_device,
        mesh=mesh,
        in_specs=(
            P("row", "layer", "col"),
            P("row", "layer", "col"),
            P(("layer", "row"), None, "col"),
            P(("layer", "row"), None, "col"),
        ),
        out_specs=P("row", "layer", "col"),
        check_vma=False,
    )
```

profile of v0, /device:TPU:32, one launch (start us, length us, event | category | flops | bytes accessed | tf_op | source)
XLA Modules:
  0.0 194.0 jit_solution(14705510479955236059)
XLA Ops:
  6.5 0.0 all-gather.3.cloned.1.call-start
  6.5 0.7 convert_bitcast_fusion.1
  7.2 0.1 broadcast_bitcast_fusion
  7.3 2.0 %bitcast_multiply_fusion = bf16[1024,256]{1,0:T(8,128)(2,1)} fusion(bf16[1024,1,256]{2,0,1:T(8,128)(2,1)} %param.4, bf16[1024]{0:T(1024)(128)(2,1)S(1)} %bitcast.29), kind=kLoop, calls=%fused_computation.8 | loop fusion | flops 262144 | bytes 1050624 | tf_op jit(solution)/shard_map/mul | solution.py:11
  9.3 0.0 all-gather.3.cloned.1.call-update
  9.3 0.0 all-gather.5.cloned.1.call-start
  9.4 0.7 convert_bitcast_fusion
  10.1 1.3 broadcast_multiply_fusion
  11.4 0.9 copy.6
  12.3 0.0 all-gather.5.cloned.1.call-update
  12.4 0.0 reduce-scatter.2.cloned.1.call-start
  12.4 62.3 %all-gather.3.cloned.1.call-done = bf16[1024,2048]{1,0:T(8,128)(2,1)} async-done(((bf16[1024,256]{1,0:T(8,128)(2,1)}), bf16[1024,2048]{1,0:T(8,128)(2,1)}) %all-gather.3.cloned.1.call-update) | async-done | bytes 4194320 | tf_op jit(solution)/shard_map/all_gather | solution.py:23
  74.7 35.0 %all-gather.5.cloned.1.call-done = bf16[2048,1024]{1,0:T(8,128)(2,1)} async-done(((bf16[256,1024]{1,0:T(8,128)(2,1)}), bf16[2048,1024]{1,0:T(8,128)(2,1)}) %all-gather.5.cloned.1.call-update) | async-done | bytes 4194320 | tf_op jit(solution)/shard_map/all_gather | solution.py:22
  109.7 7.5 %fusion.1 = f32[1024,1024]{1,0:T(8,128)S(1)} fusion(bf16[1024,2048]{1,0:T(8,128)(2,1)} %all-gather.3.cloned.1.call-done, bf16[2048,1024]{1,0:T(8,128)(2,1)} %all-gather.5.cloned.1.call-done), kind=kOutput, calls=%fused_computation.14 | convolution fusion | flops 4294967296 | bytes 12582912 | tf_op jit(solution)/shard_map/dot_general | solution.py:24
  117.2 0.4 slice_bitcast_fusion.3
  117.6 2.2 %pad_maximum_fusion = f32[4,1024,256]{2,1,0:T(8,128)} fusion(f32[1,1024,256]{2,1,0:T(8,128)S(1)} %get-tuple-element.6, f32[1,1024,256]{2,1,0:T(8,128)S(1)} %get-tuple-element.7, f32[1,1024,256]{2,1,0:T(8,128)S(1)} %get-tuple-element.8, f32[1,1024,256]{2,1,0:T(8,128)S(1)} %get-tuple-element.5), kind=kLoop, calls=%fused_computation | loop fusion | flops 3145728 | bytes 8388608 | tf_op jit(solution)/shard_map/stack | solution.py:26
  119.8 0.0 reduce-scatter.2.cloned.1.call-update
  119.8 49.5 %reduce-scatter.2.cloned.1.call-done = f32[1,1024,256]{2,1,0:T(8,128)} async-done(((f32[4,1024,256]{2,1,0:T(8,128)}), f32[1,1024,256]{2,1,0:T(8,128)}) %reduce-scatter.2.cloned.1.call-update) | async-done | bytes 1048592 | tf_op jit(solution)/shard_map/reduce_scatter | solution.py:29
  169.3 1.4 multiply_reduce_fusion
  170.7 14.6 %psum.7 = f32[1,1,256]{2,1,0:T(1,128)S(1)} all-reduce(f32[1,1,256]{2,1,0:T(1,128)S(1)} %bitcast.30), channel_id=1, replica_groups=mesh['layer'=4,'row'=8,'col'=8] {'row'}, use_global_device_ids=true, to_apply=%region_2.0 | all-reduce | flops 256 | bytes 2048 | tf_op jit(solution)/shard_map/psum | solution.py:32
  185.3 2.1 %fusion = bf16[1024,1,256]{2,0,1:T(8,128)(2,1)} fusion(f32[1,1024,256]{2,1,0:T(8,128)} %reduce-scatter.2.cloned.1.call-done, f32[256]{0:T(256)S(1)} %bitcast.31), kind=kLoop, calls=%fused_computation.6 | loop fusion | flops 786432 | bytes 1573888 | tf_op jit(solution)/shard_map/convert_element_type | solution.py:35
  (2 shorter events, 0.0 us)
Async XLA Ops:
  6.5 68.1 %all-gather.3.cloned.1.call-start = ((), (), s32[]{:S(2)}) async-start(), calls=%async_computation.1 | async-start | bytes 4718592 | tf_op jit(solution)/shard_map/all_gather | solution.py:23
  9.3 100.4 %all-gather.5.cloned.1.call-start = ((), (), s32[]{:S(2)}) async-start(), calls=%async_computation.2 | async-start | bytes 4718592 | tf_op jit(solution)/shard_map/all_gather | solution.py:22
  12.4 156.9 %reduce-scatter.2.cloned.1.call-start = ((), (), s32[]{:S(2)}) async-start(), calls=%async_computation.3 | async-start | bytes 5242880 | tf_op jit(solution)/shard_map/reduce_scatter | solution.py:29
Sparse Core Ops, SparseCore 0:
  9.5 65.1 all-gather.2
  76.5 33.1 all-gather.4
  120.0 49.2 reduce-scatter.1
where the time goes:
time: 194 us
  waiting for transfers between devices  147 us (76%)
  blocking collectives  14.6 us (8%)
  between operations  13.1 us (7%)
  other arithmetic  10.4 us (5%)
  matrix products  7.5 us (4%)
    all_gather x1, waiting for transfers between devices, per_device(): left_all = lax.all_gather(left_flat, 'col', axis=1, tiled=True)  62.3 us
    reduce_scatter x1, waiting for transfers between devices, per_device(): lax.psum_scatter(partial, 'layer', scatter_dimension=0, tiled=True)  49.5 us
    all_gather x1, waiting for transfers between devices, per_device(): right_all = lax.all_gather(right_flat, 'row', axis=0, tiled=True)  35 us
    psum x1, blocking collectives, per_device(): column = lax.psum(jnp.sum(squared, axis=0, keepdims=True), 'row')  14.6 us
    dot_general x1, matrix products, per_device(): partial = jnp.dot(left_all, right_all, preferred_element_type=jnp.float32)  7.5 us
  transfers between devices with their start and end apart: 3, of which 3 were waited for; matrix products, arithmetic and copies ran while one was open for 2% of the time, Pallas kernels for 0%

commit v1 on v0

--- a/solution.py
+++ b/solution.py
@@ -20,7 +20,10 @@
     left_flat = left_block.reshape(rows_local, columns_local)
     right_flat = right_block.reshape(right_block.shape[0], -1)
     right_all = lax.all_gather(right_flat, "row", axis=0, tiled=True)
-    left_all = lax.all_gather(left_flat, "col", axis=1, tiled=True)
+    peers = lax.axis_size("col")
+    pieces = jnp.stack([left_flat for _ in range(peers)])
+    pieces = lax.all_to_all(pieces, "col", split_axis=0, concat_axis=0)
+    left_all = jnp.concatenate(pieces, axis=1)
     partial = jnp.dot(left_all, right_all, preferred_element_type=jnp.float32)
     layers = lax.axis_size("layer")
     partial = jnp.stack(

time: 194 us -> 197 us (1.015)
  starting transfers between devices: 0.09 us -> 8.74 us
  waiting for transfers between devices: 147 us -> 140 us
  local copies, waits for them, and re-layouts: 1.42 us -> 4.07 us
  other arithmetic: 10.4 us -> 7.91 us
    all_to_all x0 -> x1, waiting for transfers between devices: none -> 93.5 us  [per_device(): pieces = lax.all_to_all(pieces, 'col', split_axis=0, concat_axis=0)]
    all_gather x1 -> x0, waiting for transfers between devices: 62.3 us -> none  [per_device(): left_all = lax.all_gather(left_flat, 'col', axis=1, tiled=True)]
    all_gather x1, waiting for transfers between devices: 35 us -> 0.01 us  [per_device(): right_all = lax.all_gather(right_flat, 'row', axis=0, tiled=True)]
    all_to_all x0 -> x1, starting transfers between devices: none -> 8.7 us  [per_device(): pieces = lax.all_to_all(pieces, 'col', split_axis=0, concat_axis=0)]
    another operation x0 -> x1, local copies, waits for them, and re-layouts: none -> 2.49 us  [per_device(): pieces = jnp.stack([left_flat for _ in range(peers)])]
    reduce_scatter x1, waiting for transfers between devices: 49.5 us -> 47 us  [per_device(): lax.psum_scatter(partial, 'layer', scatter_dimension=0, tiled=True)]
  transfers between devices with their start and end apart: 3 -> 3, of which waited for: 3 -> 2; matrix products, arithmetic and copies ran while one was open for 2% -> 1% of each run, Pallas kernels for 0% -> 0%
where the time goes in v1:
time: 197 us
  waiting for transfers between devices  140 us (71%)
  blocking collectives  14.6 us (7%)
  between operations  13.5 us (7%)
  starting transfers between devices  8.74 us (4%)
  other arithmetic  7.91 us (4%)
  matrix products  7.58 us (4%)
  local copies, waits for them, and re-layouts  4.07 us (2%)
    all_to_all x1, waiting for transfers between devices, per_device(): pieces = lax.all_to_all(pieces, 'col', split_axis=0, concat_axis=0)  93.5 us
    reduce_scatter x1, waiting for transfers between devices, per_device(): lax.psum_scatter(partial, 'layer', scatter_dimension=0, tiled=True)  47 us
    psum x1, blocking collectives, per_device(): column = lax.psum(jnp.sum(squared, axis=0, keepdims=True), 'row')  14.6 us
    all_to_all x1, starting transfers between devices, per_device(): pieces = lax.all_to_all(pieces, 'col', split_axis=0, concat_axis=0)  8.7 us
    dot_general x1, matrix products, per_device(): partial = jnp.dot(left_all, right_all, preferred_element_type=jnp.float32)  7.58 us
  transfers between devices with their start and end apart: 3, of which 2 were waited for; matrix products, arithmetic and copies ran while one was open for 1% of the time, Pallas kernels for 0%

profile of v1, /device:TPU:32, one launch (start us, length us, event | category | flops | bytes accessed | tf_op | source)
XLA Modules:
  0.0 196.9 jit_solution(403520385049782168)
XLA Ops:
  6.5 0.7 convert_bitcast_fusion.1
  7.2 0.1 broadcast_bitcast_fusion
  7.3 1.2 bitcast_multiply_fusion
  8.5 0.2 copy.5
  8.7 2.5 %stack.18 = bf16[8,1024,256]{1,2,0:T(8,128)(2,1)} broadcast(bf16[1024,256]{0,1:T(8,128)(2,1)S(1)} %copy.5), dimensions={1,2} | broadcast | bytes 4718592 | tf_op jit(solution)/shard_map/stack | solution.py:24
  11.2 0.0 copy-start.1
  11.2 0.0 copy-start
  11.2 8.7 %all-to-all-start = ((bf16[8,1024,256]{1,2,0:T(8,128)(2,1)}), bf16[8,1024,256]{1,2,0:T(8,128)(2,1)}, u32[]{:S(2)}, u32[]{:S(2)}) async-start(bf16[8,1024,256]{1,2,0:T(8,128)(2,1)} %stack.18), calls=%async_computation | async-start | bytes 8388608 | tf_op jit(solution)/shard_map/all_to_all | solution.py:25
  19.9 0.0 all-gather.2.cloned.1.call-start
  19.9 0.0 copy-done.1
  20.0 0.0 copy-done
  20.0 0.3 broadcast_multiply_fusion
  20.3 0.9 copy.7
  21.1 0.0 all-gather.2.cloned.1.call-update
  21.2 0.0 reduce-scatter.2.cloned.1.call-start
  21.2 93.5 %all-to-all-done = bf16[8,1024,256]{1,2,0:T(8,128)(2,1)} async-done(((bf16[8,1024,256]{1,2,0:T(8,128)(2,1)}), bf16[8,1024,256]{1,2,0:T(8,128)(2,1)}, u32[]{:S(2)}, u32[]{:S(2)}) %all-to-all-start) | async-done | bytes 4194336 | tf_op jit(solution)/shard_map/all_to_all | solution.py:25
  114.7 0.0 all-gather.2.cloned.1.call-done
  114.7 7.6 %fusion.1 = f32[1024,1024]{1,0:T(8,128)S(1)} fusion(bf16[1024,2048]{0,1:T(8,128)(2,1)} %bitcast.3, bf16[2048,1024]{1,0:T(8,128)(2,1)} %all-gather.2.cloned.1.call-done), kind=kOutput, calls=%fused_computation.14 | convolution fusion | flops 4294967296 | bytes 12582912 | tf_op jit(solution)/shard_map/dot_general | solution.py:27
  122.3 0.4 slice_bitcast_fusion.3
  122.7 2.2 %pad_maximum_fusion = f32[4,1024,256]{2,1,0:T(8,128)} fusion(f32[1,1024,256]{2,1,0:T(8,128)S(1)} %get-tuple-element.6, f32[1,1024,256]{2,1,0:T(8,128)S(1)} %get-tuple-element.7, f32[1,1024,256]{2,1,0:T(8,128)S(1)} %get-tuple-element.8, f32[1,1024,256]{2,1,0:T(8,128)S(1)} %get-tuple-element.5), kind=kLoop, calls=%fused_computation | loop fusion | flops 3145728 | bytes 8388608 | tf_op jit(solution)/shard_map/stack | solution.py:29
  124.9 0.0 reduce-scatter.2.cloned.1.call-update
  124.9 47.0 %reduce-scatter.2.cloned.1.call-done = f32[1,1024,256]{2,1,0:T(8,128)} async-done(((f32[4,1024,256]{2,1,0:T(8,128)}), f32[1,1024,256]{2,1,0:T(8,128)}) %reduce-scatter.2.cloned.1.call-update) | async-done | bytes 1048592 | tf_op jit(solution)/shard_map/reduce_scatter | solution.py:32
  171.9 1.4 multiply_reduce_fusion
  173.3 14.6 %psum.7 = f32[1,1,256]{2,1,0:T(1,128)S(1)} all-reduce(f32[1,1,256]{2,1,0:T(1,128)S(1)} %bitcast.33), channel_id=1, replica_groups=mesh['layer'=4,'row'=8,'col'=8] {'row'}, use_global_device_ids=true, to_apply=%region_2.0 | all-reduce | flops 256 | bytes 2048 | tf_op jit(solution)/shard_map/psum | solution.py:35
  187.9 2.1 %fusion = bf16[1024,1,256]{2,0,1:T(8,128)(2,1)} fusion(f32[1,1024,256]{2,1,0:T(8,128)} %reduce-scatter.2.cloned.1.call-done, f32[256]{0:T(256)S(1)} %bitcast.34), kind=kLoop, calls=%fused_computation.6 | loop fusion | flops 786432 | bytes 1573888 | tf_op jit(solution)/shard_map/convert_element_type | solution.py:38
  (3 shorter events, 0.0 us)
Async XLA Ops:
  11.2 8.7 %copy-start.1 = (s32[1,4,1]{1,2,0:T(1,128)S(1)}, s32[1,4,1]{1,2,0:T(1,128)}, u32[]{:S(2)}) copy-start(s32[1,4,1]{1,2,0:T(1,128)} %param.7) | copy-start | bytes 52
  11.2 8.7 %copy-start = (bf16[256,4,256]{2,1,0:T(4,128)(2,1)S(1)}, bf16[256,4,256]{2,1,0:T(4,128)(2,1)}, u32[]{:S(2)}) copy-start(bf16[256,4,256]{2,1,0:T(4,128)(2,1)} %param.6) | copy-start | bytes 1572868
  11.2 103.5 %all-to-all-start = ((bf16[8,1024,256]{1,2,0:T(8,128)(2,1)}), bf16[8,1024,256]{1,2,0:T(8,128)(2,1)}, u32[]{:S(2)}, u32[]{:S(2)}) async-start(bf16[8,1024,256]{1,2,0:T(8,128)(2,1)} %stack.18), calls=%async_computation | async-start | bytes 8388608 | tf_op jit(solution)/shard_map/all_to_all | solution.py:25
  19.9 94.8 %all-gather.2.cloned.1.call-start = ((), (), s32[]{:S(2)}) async-start(), calls=%async_computation.2 | async-start | bytes 4718592 | tf_op jit(solution)/shard_map/all_gather | solution.py:22
  21.2 150.7 %reduce-scatter.2.cloned.1.call-start = ((), (), s32[]{:S(2)}) async-start(), calls=%async_computation.3 | async-start | bytes 5242880 | tf_op jit(solution)/shard_map/reduce_scatter | solution.py:32
Sparse Core Ops, SparseCore 0:
  22.6 35.9 all-gather.1
  125.1 46.7 reduce-scatter.1

commit v2 on v0

--- a/solution.py
+++ b/solution.py
@@ -19,7 +19,11 @@
     columns_local = left_block.shape[2]
     left_flat = left_block.reshape(rows_local, columns_local)
     right_flat = right_block.reshape(right_block.shape[0], -1)
-    right_all = lax.all_gather(right_flat, "row", axis=0, tiled=True)
+    size = lax.axis_size("row")
+    repeats = [size if d == 0 else 1 for d in range(right_flat.ndim)]
+    right_all = lax.all_to_all(
+        jnp.tile(right_flat, repeats), "row", split_axis=0, concat_axis=0, tiled=True
+    )
     left_all = lax.all_gather(left_flat, "col", axis=1, tiled=True)
     partial = jnp.dot(left_all, right_all, preferred_element_type=jnp.float32)
     layers = lax.axis_size("layer")

time: 194 us -> 158 us (0.81)
  waiting for transfers between devices: 147 us -> 55.9 us
  blocking collectives: 14.6 us -> 69.4 us
    all_to_all x0 -> x1, blocking collectives: none -> 54.7 us  [per_device(): lax.all_to_all(jnp.tile(right_flat, repeats), 'row', split_axis=0, concat...]
    all_gather x1, waiting for transfers between devices: 62.3 us -> 7.55 us  [per_device(): left_all = lax.all_gather(left_flat, 'col', axis=1, tiled=True)]
    all_gather x1 -> x0, waiting for transfers between devices: 35 us -> none  [per_device(): right_all = lax.all_gather(right_flat, 'row', axis=0, tiled=True)]
  transfers between devices with their start and end apart: 3 -> 2, of which waited for: 3 -> 2; matrix products, arithmetic and copies ran while one was open for 2% -> 2% of each run, Pallas kernels for 0% -> 0%
where the time goes in v2:
time: 158 us
  blocking collectives  69.4 us (44%)
  waiting for transfers between devices  55.9 us (35%)
  between operations  13.4 us (8%)
  other arithmetic  10.4 us (7%)
  matrix products  7.5 us (5%)
    all_to_all x1, blocking collectives, per_device(): lax.all_to_all(jnp.tile(right_flat, repeats), 'row', split_axis=0, concat...  54.7 us
    reduce_scatter x1, waiting for transfers between devices, per_device(): lax.psum_scatter(partial, 'layer', scatter_dimension=0, tiled=True)  48.3 us
    psum x1, blocking collectives, per_device(): column = lax.psum(jnp.sum(squared, axis=0, keepdims=True), 'row')  14.7 us
    all_gather x1, waiting for transfers between devices, per_device(): left_all = lax.all_gather(left_flat, 'col', axis=1, tiled=True)  7.55 us
    dot_general x1, matrix products, per_device(): partial = jnp.dot(left_all, right_all, preferred_element_type=jnp.float32)  7.5 us
    mul x2, other arithmetic, expand_tiles(): blocks = blocks * pattern[:, None, :, :, None].astype(values.dtype)  3.37 us
  transfers between devices with their start and end apart: 2, of which 2 were waited for; matrix products, arithmetic and copies ran while one was open for 2% of the time, Pallas kernels for 0%

profile of v2, /device:TPU:32, one launch (start us, length us, event | category | flops | bytes accessed | tf_op | source)
XLA Modules:
  0.0 157.7 jit_solution(4230839220704612140)
XLA Ops:
  6.5 0.0 all-gather.2.cloned.1.call-start
  6.5 0.7 convert_bitcast_fusion.1
  7.2 0.1 broadcast_bitcast_fusion
  7.3 2.0 %bitcast_multiply_fusion = bf16[1024,256]{1,0:T(8,128)(2,1)} fusion(bf16[1024,1,256]{2,0,1:T(8,128)(2,1)} %param.4, bf16[1024]{0:T(1024)(128)(2,1)S(1)} %bitcast.31), kind=kLoop, calls=%fused_computation.8 | loop fusion | flops 262144 | bytes 1050624 | tf_op jit(solution)/shard_map/mul | solution.py:11
  9.3 0.0 all-gather.2.cloned.1.call-update
  9.3 0.0 reduce-scatter.2.cloned.1.call-start
  9.4 0.7 convert_bitcast_fusion
  10.1 1.3 broadcast_multiply_fusion
  11.4 0.1 copy.6
  11.5 0.5 tile.9
  12.0 54.7 %all_to_all.9 = bf16[8,256,1024]{2,1,0:T(8,128)(2,1)} all-to-all(bf16[8,256,1024]{2,1,0:T(8,128)(2,1)S(1)} %tile.9), channel_id=1, replica_groups=mesh['layer'=4,'row'=8,'col'=8] {'row'}, dimensions={0} | all-to-all | bytes 8388608 | tf_op jit(solution)/shard_map/all_to_all | solution.py:24
  66.7 7.6 %all-gather.2.cloned.1.call-done = bf16[1024,2048]{1,0:T(8,128)(2,1)} async-done(((bf16[1024,256]{1,0:T(8,128)(2,1)}), bf16[1024,2048]{1,0:T(8,128)(2,1)}) %all-gather.2.cloned.1.call-update) | async-done | bytes 4194320 | tf_op jit(solution)/shard_map/all_gather | solution.py:27
  74.3 7.5 %fusion.1 = f32[1024,1024]{1,0:T(8,128)S(1)} fusion(bf16[1024,2048]{1,0:T(8,128)(2,1)} %all-gather.2.cloned.1.call-done, bf16[2048,1024]{1,0:T(8,128)(2,1)} %bitcast.28), kind=kOutput, calls=%fused_computation.14 | convolution fusion | flops 4294967296 | bytes 12582912 | tf_op jit(solution)/shard_map/dot_general | solution.py:28
  81.8 0.4 slice_bitcast_fusion.3
  82.2 2.2 %pad_maximum_fusion = f32[4,1024,256]{2,1,0:T(8,128)} fusion(f32[1,1024,256]{2,1,0:T(8,128)S(1)} %get-tuple-element.6, f32[1,1024,256]{2,1,0:T(8,128)S(1)} %get-tuple-element.7, f32[1,1024,256]{2,1,0:T(8,128)S(1)} %get-tuple-element.8, f32[1,1024,256]{2,1,0:T(8,128)S(1)} %get-tuple-element.5), kind=kLoop, calls=%fused_computation | loop fusion | flops 3145728 | bytes 8388608 | tf_op jit(solution)/shard_map/stack | solution.py:30
  84.4 0.0 reduce-scatter.2.cloned.1.call-update
  84.4 48.3 %reduce-scatter.2.cloned.1.call-done = f32[1,1024,256]{2,1,0:T(8,128)} async-done(((f32[4,1024,256]{2,1,0:T(8,128)}), f32[1,1024,256]{2,1,0:T(8,128)}) %reduce-scatter.2.cloned.1.call-update) | async-done | bytes 1048592 | tf_op jit(solution)/shard_map/reduce_scatter | solution.py:33
  132.7 1.4 multiply_reduce_fusion
  134.1 14.7 %psum.7 = f32[1,1,256]{2,1,0:T(1,128)S(1)} all-reduce(f32[1,1,256]{2,1,0:T(1,128)S(1)} %bitcast.32), channel_id=1, replica_groups=mesh['layer'=4,'row'=8,'col'=8] {'row'}, use_global_device_ids=true, to_apply=%region_2.0 | all-reduce | flops 256 | bytes 2048 | tf_op jit(solution)/shard_map/psum | solution.py:36
  148.8 2.1 %fusion = bf16[1024,1,256]{2,0,1:T(8,128)(2,1)} fusion(f32[1,1024,256]{2,1,0:T(8,128)} %reduce-scatter.2.cloned.1.call-done, f32[256]{0:T(256)S(1)} %bitcast.33), kind=kLoop, calls=%fused_computation.6 | loop fusion | flops 786432 | bytes 1573888 | tf_op jit(solution)/shard_map/convert_element_type | solution.py:39
  (2 shorter events, 0.0 us)
Async XLA Ops:
  6.5 67.7 %all-gather.2.cloned.1.call-start = ((), (), s32[]{:S(2)}) async-start(), calls=%async_computation.2 | async-start | bytes 4718592 | tf_op jit(solution)/shard_map/all_gather | solution.py:27
  9.3 123.4 %reduce-scatter.2.cloned.1.call-start = ((), (), s32[]{:S(2)}) async-start(), calls=%async_computation.3 | async-start | bytes 5242880 | tf_op jit(solution)/shard_map/reduce_scatter | solution.py:33
Sparse Core Ops, SparseCore 0:
  9.5 64.7 all-gather.1
  84.5 48.1 reduce-scatter.1
